TPU v7x, 32 devices: a whole 2x2x4 slice. The times are simulated.
32 devices in a mesh: fsdp: 2 (over y), ctx: 4 (over x, core), tp: 4 (over z).
Axes of the slice: x: 2, y: 2, z: 4, core: 2. Of those that a mesh axis runs over, the one named last changes fastest.
Arguments:
- tokens: bfloat16 [8, 2048, 1024], P('fsdp', 'ctx'), may hold values from -6 to 6
- segments: int32 [8, 2048], P('fsdp'), may hold values from 0 to 10, as said below
- w_qkv: bfloat16 [3, 1024, 1024], P(None, 'fsdp', 'tp'), may hold values from -0.1875 to 0.1875
- b_qv: bfloat16 [2, 16, 64], P(None, 'tp', 'fsdp'), may hold values from -3 to 3
- w_o: bfloat16 [1024, 1024], P('tp', 'fsdp'), may hold values from -3 to 3
- b_o: bfloat16 [1024], P('fsdp'), may hold values from -3 to 3
- ln1_gain: bfloat16 [1024], P('fsdp'), may hold values from 0.5 to 1.5
- ln1_bias: bfloat16 [1024], P('fsdp'), may hold values from -2 to 2
- w_in: bfloat16 [1024, 4096], P('fsdp', 'tp'), may hold values from -0.1875 to 0.1875
- b_in: bfloat16 [64, 64], P('tp', 'fsdp'), may hold values from -3 to 3
- w_out: bfloat16 [4096, 1024], P('tp', 'fsdp'), may hold values from -0.09375 to 0.09375
- b_out: bfloat16 [1024], P('fsdp'), may hold values from -3 to 3
- ln2_gain: bfloat16 [1024], P('fsdp'), may hold values from 0.5 to 1.5
- ln2_bias: bfloat16 [1024], P('fsdp'), may hold values from -2 to 2
- cotangent: bfloat16 [8, 2048, 1024], P('fsdp', 'ctx'), may hold values from -6 to 6
Outputs:
- output: bfloat16 [8, 2048, 1024], P('fsdp', 'ctx')
- grad_tokens: bfloat16 [8, 2048, 1024], P('fsdp', 'ctx')
- grad_w_qkv: float32 [3, 1024, 1024], P(None, 'fsdp', 'tp')
- grad_b_qv: float32 [2, 16, 64], P(None, 'tp', 'fsdp')
- grad_w_o: float32 [1024, 1024], P('tp', 'fsdp')
- grad_b_o: float32 [1024], P('fsdp')
- grad_ln1_gain: float32 [1024], P('fsdp')
- grad_ln1_bias: float32 [1024], P('fsdp')
- grad_w_in: float32 [1024, 4096], P('fsdp', 'tp')
- grad_b_in: float32 [64, 64], P('tp', 'fsdp')
- grad_w_out: float32 [4096, 1024], P('tp', 'fsdp')
- grad_b_out: float32 [1024], P('fsdp')
- grad_ln2_gain: float32 [1024], P('fsdp')
- grad_ln2_bias: float32 [1024], P('fsdp')
Inputs may be any that keep to these rules, and one draw needn't show every extreme that they name: `segments`: in each sequence the ids start at 0 and rise by one at each document boundary; every document has 200 to 2000 tokens except a sequence's last, which ends with the sequence and may be shorter; one document of the batch has exactly 2000 tokens, and one sequence is made of documents of exactly 200 tokens except its last.
All inputs are finite; a program needn't handle non-finite values.
Results may differ from a plain program's by a relative error of at most 0.02.
Values may be sent and summed in bfloat16 or wider, within the bound.
No kernel may reach another device: no remote copies, remote signals or barrier semaphores. Data moves between devices by JAX's collectives and lax.ppermute only.
A program may use at most 192 MiB of HBM per device.

v0:
```python
import jax
import jax.numpy as jnp
from jax import lax
from jax.sharding import PartitionSpec as P

EPSILON = 1e-12
NEG_LARGE = -1e30
SCALE_QK = 0.125


def layer_norm(values, gain_vec, offset):
    center = values - jnp.mean(values, -1, keepdims=True)
    spread = jnp.mean(center * center, -1, keepdims=True)
    return center * lax.rsqrt(spread + EPSILON) * gain_vec + offset


def gelu_exact(values):
    return 0.5 * values * (1.0 + jax.scipy.special.erf(values * 0.7071067811865476))


def to_heads(blocks, head_size):
    seq_count, row_len, col_count = blocks.shape
    return blocks.reshape(seq_count, row_len, col_count // head_size, head_size).transpose(
        2, 0, 1, 3
    )


def from_heads(blocks):
    head_count, seq_count, row_len, head_size = blocks.shape
    return blocks.transpose(1, 2, 0, 3).reshape(seq_count, row_len, head_count * head_size)


def masked_scores(query_head, key_head, same_doc):
    scores = (
        jnp.einsum("sqd,skd->sqk", query_head, key_head, preferred_element_type=jnp.float32)
        * SCALE_QK
    )
    return jnp.where(same_doc, scores, NEG_LARGE)


def local(
    tokens,
    segments,
    w_qkv,
    b_qv,
    w_o,
    b_o,
    ln1_gain,
    ln1_bias,
    w_in,
    b_in,
    w_out,
    b_out,
    ln2_gain,
    ln2_bias,
    cotangent,
):
    seq_count, local_len, model_width = tokens.shape
    (
        proj_qkv,
        bias_qv,
        proj_attn,
        bias_attn,
        gain_first,
        shift_first,
        proj_in,
        bias_in,
        proj_out,
        bias_out,
        gain_second,
        shift_second,
    ) = (
        lax.all_gather(w_qkv, "fsdp", axis=1, tiled=True),
        lax.all_gather(b_qv, "fsdp", axis=2, tiled=True),
        lax.all_gather(w_o, "fsdp", axis=1, tiled=True),
        lax.all_gather(b_o, "fsdp", axis=0, tiled=True),
        lax.all_gather(ln1_gain, "fsdp", axis=0, tiled=True),
        lax.all_gather(ln1_bias, "fsdp", axis=0, tiled=True),
        lax.all_gather(w_in, "fsdp", axis=0, tiled=True),
        lax.all_gather(b_in, "fsdp", axis=1, tiled=True),
        lax.all_gather(w_out, "fsdp", axis=1, tiled=True),
        lax.all_gather(b_out, "fsdp", axis=0, tiled=True),
        lax.all_gather(ln2_gain, "fsdp", axis=0, tiled=True),
        lax.all_gather(ln2_bias, "fsdp", axis=0, tiled=True),
    )
    local_width = proj_qkv.shape[2]
    head_size = bias_qv.shape[2]
    local_heads = local_width // head_size
    row_count = seq_count * local_len
    inputs = tokens.reshape(row_count, model_width)
    gain_one = gain_first.astype(jnp.float32)
    shift_one = shift_first.astype(jnp.float32)
    gain_two = gain_second.astype(jnp.float32)
    shift_two = shift_second.astype(jnp.float32)

    def finish_sum(partial_rows):
        return lax.psum(partial_rows.astype(jnp.bfloat16), "tp").astype(jnp.float32)

    projected = jnp.einsum("rd,kdc->krc", inputs, proj_qkv, preferred_element_type=jnp.float32)
    query_rows = (projected[0] + bias_qv[0].reshape(-1).astype(jnp.float32)).astype(jnp.bfloat16)
    key_blocks = projected[1].astype(jnp.bfloat16).reshape(seq_count, local_len, local_width)
    value_blocks = (
        (projected[2] + bias_qv[1].reshape(-1).astype(jnp.float32))
        .astype(jnp.bfloat16)
        .reshape(seq_count, local_len, local_width)
    )
    key_all, value_all = (
        lax.all_gather(key_blocks, "ctx", axis=1, tiled=True),
        lax.all_gather(value_blocks, "ctx", axis=1, tiled=True),
    )
    block_start = lax.axis_index("ctx") * local_len
    query_segments = lax.dynamic_slice_in_dim(segments, block_start, local_len, 1)
    same_doc = query_segments[:, :, None] == segments[:, None, :]
    query_heads = to_heads(query_rows.reshape(seq_count, local_len, local_width), head_size)
    key_heads = to_heads(key_all, head_size)
    value_heads = to_heads(value_all, head_size)

    def attend_head(operands):
        query_head, key_head, value_head = operands
        scores = masked_scores(query_head, key_head, same_doc)
        row_max = jnp.max(scores, -1, keepdims=True)
        exp_scores = jnp.exp(scores - row_max)
        denominator = jnp.sum(exp_scores, -1, keepdims=True)
        probs_low = (exp_scores / denominator).astype(jnp.bfloat16)
        mixed_rows = jnp.einsum(
            "sqk,skd->sqd", probs_low, value_head, preferred_element_type=jnp.float32
        )
        return (mixed_rows.astype(jnp.bfloat16), row_max, denominator)

    attended_heads, row_maxes, denominators = lax.map(
        attend_head, (query_heads, key_heads, value_heads)
    )
    attended_rows = from_heads(attended_heads).reshape(row_count, local_width)
    attn_part = jnp.dot(attended_rows, proj_attn, preferred_element_type=jnp.float32)
    attn_rows = finish_sum(attn_part) + bias_attn.astype(jnp.float32)
    first_in = inputs.astype(jnp.float32) + attn_rows
    normed = layer_norm(first_in, gain_one, shift_one)
    normed_low = normed.astype(jnp.bfloat16)
    pre_act = jnp.dot(normed_low, proj_in, preferred_element_type=jnp.float32) + bias_in.reshape(
        -1
    ).astype(jnp.float32)
    act_low = gelu_exact(pre_act).astype(jnp.bfloat16)
    mlp_part = jnp.dot(act_low, proj_out, preferred_element_type=jnp.float32)
    mlp_rows = finish_sum(mlp_part) + bias_out.astype(jnp.float32)
    second_in = normed + mlp_rows
    final_rows = layer_norm(second_in, gain_two, shift_two)
    output = final_rows.astype(jnp.bfloat16).reshape(seq_count, local_len, model_width)
    grad_final = cotangent.reshape(row_count, model_width).astype(jnp.float32)
    unused_second, pull_second = jax.vjp(layer_norm, second_in, gain_two, shift_two)
    grad_second, grad_gain_second, grad_shift_second = pull_second(grad_final)
    grad_mlp = grad_second.astype(jnp.bfloat16)
    grad_bias_out = jnp.sum(grad_mlp, 0, dtype=jnp.float32)
    grad_proj_out = jnp.einsum("rf,rd->fd", act_low, grad_mlp, preferred_element_type=jnp.float32)
    grad_act = jnp.einsum("rd,fd->rf", grad_mlp, proj_out, preferred_element_type=jnp.float32)
    unused_gelu, pull_gelu = jax.vjp(gelu_exact, pre_act)
    grad_pre = pull_gelu(grad_act)[0].astype(jnp.bfloat16)
    grad_bias_in = jnp.sum(grad_pre, 0, dtype=jnp.float32).reshape(bias_in.shape)
    grad_proj_in = jnp.einsum("rd,rf->df", normed_low, grad_pre, preferred_element_type=jnp.float32)
    back_part = jnp.einsum("rf,df->rd", grad_pre, proj_in, preferred_element_type=jnp.float32)
    grad_normed = grad_second + finish_sum(back_part)
    unused_first, pull_first = jax.vjp(layer_norm, first_in, gain_one, shift_one)
    grad_first, grad_gain_first, grad_shift_first = pull_first(grad_normed)
    grad_attn = grad_first.astype(jnp.bfloat16)
    grad_bias_attn = jnp.sum(grad_attn, 0, dtype=jnp.float32)
    grad_proj_attn = jnp.einsum(
        "rc,rd->cd", attended_rows, grad_attn, preferred_element_type=jnp.float32
    )
    grad_attended = jnp.einsum(
        "rd,cd->rc", grad_attn, proj_attn, preferred_element_type=jnp.float32
    ).astype(jnp.bfloat16)
    grad_att_heads = to_heads(grad_attended.reshape(seq_count, local_len, local_width), head_size)
    key_again, value_again = (
        lax.all_gather(key_blocks, "ctx", axis=1, tiled=True),
        lax.all_gather(value_blocks, "ctx", axis=1, tiled=True),
    )
    key_back = to_heads(key_again, head_size)
    value_back = to_heads(value_again, head_size)

    def head_grads(operands):
        query_head, key_head, value_head, grad_head, row_max, denominator = operands
        scores = masked_scores(query_head, key_head, same_doc)
        attn_probs = jnp.exp(scores - row_max) / denominator
        probs_low = attn_probs.astype(jnp.bfloat16)
        grad_probs = jnp.einsum(
            "sqd,skd->sqk", grad_head, value_head, preferred_element_type=jnp.float32
        )
        row_delta = jnp.sum(attn_probs * grad_probs, -1, keepdims=True)
        grad_scores = (attn_probs * (grad_probs - row_delta)).astype(jnp.bfloat16)
        grad_query = (
            jnp.einsum("sqk,skd->sqd", grad_scores, key_head, preferred_element_type=jnp.float32)
            * SCALE_QK
        )
        grad_key = (
            jnp.einsum("sqk,sqd->skd", grad_scores, query_head, preferred_element_type=jnp.float32)
            * SCALE_QK
        )
        grad_value = jnp.einsum(
            "sqk,sqd->skd", probs_low, grad_head, preferred_element_type=jnp.float32
        )
        return (grad_query.astype(jnp.bfloat16), grad_key, grad_value)

    grad_query_heads, grad_key_heads, grad_value_heads = lax.map(
        head_grads, (query_heads, key_back, value_back, grad_att_heads, row_maxes, denominators)
    )
    grad_key_full = from_heads(grad_key_heads)
    grad_value_full = from_heads(grad_value_heads)
    grad_key_part, grad_value_part = (
        lax.psum_scatter(
            grad_key_full.astype(jnp.bfloat16), "ctx", scatter_dimension=1, tiled=True
        ).astype(jnp.float32),
        lax.psum_scatter(
            grad_value_full.astype(jnp.bfloat16), "ctx", scatter_dimension=1, tiled=True
        ).astype(jnp.float32),
    )
    grad_query_rows = from_heads(grad_query_heads).reshape(row_count, local_width)
    grad_key_rows = grad_key_part.astype(jnp.bfloat16).reshape(row_count, local_width)
    grad_value_rows = grad_value_part.astype(jnp.bfloat16).reshape(row_count, local_width)
    grad_stack = jnp.stack([grad_query_rows, grad_key_rows, grad_value_rows])
    grad_proj_qkv = jnp.einsum(
        "rd,krc->kdc", inputs, grad_stack, preferred_element_type=jnp.float32
    )
    grad_bias_qv = jnp.stack(
        [
            jnp.sum(grad_query_rows, 0, dtype=jnp.float32),
            jnp.sum(grad_value_rows, 0, dtype=jnp.float32),
        ]
    ).reshape(2, local_heads, head_size)
    input_part = jnp.einsum("krc,kdc->rd", grad_stack, proj_qkv, preferred_element_type=jnp.float32)
    grad_inputs = grad_first + finish_sum(input_part)
    grad_tokens = grad_inputs.astype(jnp.bfloat16).reshape(seq_count, local_len, model_width)
    (
        share_qkv,
        share_bqv,
        share_attn,
        share_battn,
        share_gone,
        share_sone,
        share_in,
        share_bin,
        share_out,
        share_bout,
        share_gtwo,
        share_stwo,
    ) = (
        lax.psum_scatter(grad_proj_qkv, ("fsdp", "ctx"), scatter_dimension=1, tiled=True),
        lax.psum_scatter(grad_bias_qv, ("fsdp", "ctx"), scatter_dimension=2, tiled=True),
        lax.psum_scatter(grad_proj_attn, ("fsdp", "ctx"), scatter_dimension=1, tiled=True),
        lax.psum_scatter(grad_bias_attn, ("fsdp", "ctx"), scatter_dimension=0, tiled=True),
        lax.psum_scatter(grad_gain_first, ("fsdp", "ctx"), scatter_dimension=0, tiled=True),
        lax.psum_scatter(grad_shift_first, ("fsdp", "ctx"), scatter_dimension=0, tiled=True),
        lax.psum_scatter(grad_proj_in, ("fsdp", "ctx"), scatter_dimension=0, tiled=True),
        lax.psum_scatter(grad_bias_in, ("fsdp", "ctx"), scatter_dimension=1, tiled=True),
        lax.psum_scatter(grad_proj_out, ("fsdp", "ctx"), scatter_dimension=1, tiled=True),
        lax.psum_scatter(grad_bias_out, ("fsdp", "ctx"), scatter_dimension=0, tiled=True),
        lax.psum_scatter(grad_gain_second, ("fsdp", "ctx"), scatter_dimension=0, tiled=True),
        lax.psum_scatter(grad_shift_second, ("fsdp", "ctx"), scatter_dimension=0, tiled=True),
    )
    reduced = (
        lax.all_gather(share_qkv.astype(jnp.bfloat16), "ctx", axis=1, tiled=True).astype(
            share_qkv.dtype
        ),
        lax.all_gather(share_bqv.astype(jnp.bfloat16), "ctx", axis=2, tiled=True).astype(
            share_bqv.dtype
        ),
        lax.all_gather(share_attn.astype(jnp.bfloat16), "ctx", axis=1, tiled=True).astype(
            share_attn.dtype
        ),
        lax.all_gather(share_battn.astype(jnp.bfloat16), "ctx", axis=0, tiled=True).astype(
            share_battn.dtype
        ),
        lax.all_gather(share_gone.astype(jnp.bfloat16), "ctx", axis=0, tiled=True).astype(
            share_gone.dtype
        ),
        lax.all_gather(share_sone.astype(jnp.bfloat16), "ctx", axis=0, tiled=True).astype(
            share_sone.dtype
        ),
        lax.all_gather(share_in.astype(jnp.bfloat16), "ctx", axis=0, tiled=True).astype(
            share_in.dtype
        ),
        lax.all_gather(share_bin.astype(jnp.bfloat16), "ctx", axis=1, tiled=True).astype(
            share_bin.dtype
        ),
        lax.all_gather(share_out.astype(jnp.bfloat16), "ctx", axis=1, tiled=True).astype(
            share_out.dtype
        ),
        lax.all_gather(share_bout.astype(jnp.bfloat16), "ctx", axis=0, tiled=True).astype(
            share_bout.dtype
        ),
        lax.all_gather(share_gtwo.astype(jnp.bfloat16), "ctx", axis=0, tiled=True).astype(
            share_gtwo.dtype
        ),
        lax.all_gather(share_stwo.astype(jnp.bfloat16), "ctx", axis=0, tiled=True).astype(
            share_stwo.dtype
        ),
    )
    return (
        output,
        grad_tokens,
        reduced[0],
        reduced[1],
        reduced[2],
        reduced[3],
        reduced[4],
        reduced[5],
        reduced[6],
        reduced[7],
        reduced[8],
        reduced[9],
        reduced[10],
        reduced[11],
    )


def solution(mesh):
    in_specs = (
        P("fsdp", "ctx", None),
        P("fsdp", None),
        P(None, "fsdp", "tp"),
        P(None, "tp", "fsdp"),
        P("tp", "fsdp"),
        P("fsdp"),
        P("fsdp"),
        P("fsdp"),
        P("fsdp", "tp"),
        P("tp", "fsdp"),
        P("tp", "fsdp"),
        P("fsdp"),
        P("fsdp"),
        P("fsdp"),
        P("fsdp", "ctx", None),
    )
    out_specs = (
        P("fsdp", "ctx", None),
        P("fsdp", "ctx", None),
        P(None, "fsdp", "tp"),
        P(None, "tp", "fsdp"),
        P("tp", "fsdp"),
        P("fsdp"),
        P("fsdp"),
        P("fsdp"),
        P("fsdp", "tp"),
        P("tp", "fsdp"),
        P("tp", "fsdp"),
        P("fsdp"),
        P("fsdp"),
        P("fsdp"),
    )
    return jax.shard_map(local, mesh=mesh, in_specs=in_specs, out_specs=out_specs, check_vma=False)
```

profile of v0, /device:TPU:0, one launch (start us, length us, event | category | flops | bytes accessed | tf_op | source)
XLA Modules:
  0.0 1384.4 jit_solution(14793995309170661180)
XLA Ops:
  16.0 24.1 %all-gather.21.cloned.1.call-done = bf16[3,1024,256]{1,2,0:T(8,128)(2,1)} async-done(((bf16[3,512,256]{1,2,0:T(8,128)(2,1)}), bf16[3,1024,256]{1,2,0:T(8,128)(2,1)}) %all-gather.21.cloned.1.call-update) | async-done | bytes 1572880 | tf_op jit(solution)/shard_map/all_gather | solution.py:73
  71.3 17.5 %all-gather.25.cloned.1.call-done = bf16[4,2048,256]{1,2,0:T(8,128)(2,1)} async-done(((bf16[4,512,256]{1,2,0:T(8,128)(2,1)}), bf16[4,2048,256]{1,2,0:T(8,128)(2,1)}) %all-gather.25.cloned.1.call-update) | async-done | bytes 4194320 | tf_op jit(solution)/shard_map/all_gather | solution.py:109
  93.5 31.9 %all-gather.23.cloned.1.call-done = bf16[4,2048,256]{1,2,0:T(8,128)(2,1)} async-done(((bf16[4,512,256]{1,2,0:T(8,128)(2,1)}), bf16[4,2048,256]{1,2,0:T(8,128)(2,1)}) %all-gather.23.cloned.1.call-update) | async-done | bytes 4194320 | tf_op jit(solution)/shard_map/all_gather | solution.py:108
  130.3 62.6 %while.30 = (s32[]{:T(128)}, bf16[4,4,512,64]{2,3,1,0:T(8,128)(2,1)S(1)}, f32[4,4,512,1]{2,1,3,0:T(4,128)}, f32[4,4,512,1]{2,1,3,0:T(4,128)}, bf16[4,4,512,64]{2...) while((s32[]{:T(128)}, ...), condition=%wide.region_3.4_spmd.clone, body=%wide.region_0.3_spmd.clone.sunk | while | flops 1136783360 | bytes 53152356 | solution.py:130
  217.5 136.0 %all-reduce.14.cloned.1.call-done = bf16[2048,1024]{1,0:T(8,128)(2,1)} async-done(((bf16[2048,1024]{1,0:T(8,128)(2,1)}), bf16[2048,1024]{1,0:T(8,128)(2,1)}) %all-reduce.14.cloned.1.call-update) | async-done | bytes 4194320 | tf_op jit(solution)/shard_map/psum | solution.py:97
  364.1 22.9 %all-gather.27.cloned.1.call-done = bf16[1024,1024]{1,0:T(8,128)(2,1)} async-done(((bf16[512,1024]{1,0:T(8,128)(2,1)}), bf16[1024,1024]{1,0:T(8,128)(2,1)}) %all-gather.27.cloned.1.call-update) | async-done | bytes 2097168 | tf_op jit(solution)/shard_map/all_gather | solution.py:79
  387.0 11.0 multiply_convert_fusion.1
  398.0 23.6 %all-gather.29.cloned.1.call-done = bf16[1024,1024]{1,0:T(8,128)(2,1)} async-done(((bf16[1024,512]{1,0:T(8,128)(2,1)}), bf16[1024,1024]{1,0:T(8,128)(2,1)}) %all-gather.29.cloned.1.call-update) | async-done | bytes 2097168 | tf_op jit(solution)/shard_map/all_gather | solution.py:81
  444.7 141.4 %all-reduce.16.cloned.1.call-done = bf16[2048,1024]{1,0:T(8,128)(2,1)} async-done(((bf16[2048,1024]{1,0:T(8,128)(2,1)}), bf16[2048,1024]{1,0:T(8,128)(2,1)}) %all-reduce.16.cloned.1.call-update) | async-done | bytes 4194320 | tf_op jit(solution)/shard_map/psum | solution.py:97
  606.5 12.3 convert_reduce_fusion.2
  627.3 10.0 fusion.81
  637.4 11.4 fusion.69
  648.9 132.4 %all-reduce.18.cloned.1.call-done = bf16[2048,1024]{1,0:T(8,128)(2,1)} async-done(((bf16[2048,1024]{1,0:T(8,128)(2,1)}), bf16[2048,1024]{1,0:T(8,128)(2,1)}) %all-reduce.18.cloned.1.call-update) | async-done | bytes 4194320 | tf_op jit(solution)/shard_map/psum | solution.py:97
  810.9 182.2 %while.31 = (s32[]{:T(128)}, bf16[4,4,512,64]{2,3,1,0:T(8,128)(2,1)}, bf16[4,4,2048,64]{2,3,0,1:T(8,128)(2,1)}, bf16[4,4,2048,64]{2,3,0,1:T(8,128)(2,1)}, bf16[4...) while((s32[]{:T(128)}, ...), condition=%wide.region_17.18_spmd.clone, body=%wide.region_15.17_spmd.clone.sunk | while | flops 2731276288 | bytes 202223824 | solution.py:202
  822.3 9.8 multiply_reduce_fusion.6
  868.4 9.8 multiply_reduce_fusion.6
  1007.2 29.6 %reduce-scatter.9.cloned.1.call-done = bf16[4,512,256]{1,2,0:T(8,128)(2,1)} async-done(((bf16[4,2048,256]{1,2,0:T(8,128)(2,1)}), bf16[4,512,256]{1,2,0:T(8,128)(2,1)}) %reduce-scatter.9.cloned.1.call-update) | async-done | bytes 1048592 | tf_op jit(solution)/shard_map/reduce_scatter | solution.py:208
  1038.3 45.3 %reduce-scatter.11.cloned.1.call-done = bf16[4,512,256]{1,2,0:T(8,128)(2,1)} async-done(((bf16[4,2048,256]{1,2,0:T(8,128)(2,1)}), bf16[4,512,256]{1,2,0:T(8,128)(2,1)}) %reduce-scatter.11.cloned.1.call-update) | async-done | bytes 1048592 | tf_op jit(solution)/shard_map/reduce_scatter | solution.py:211
  1105.4 18.0 %reduce-scatter.15.cloned.1.call-done = f32[256,128]{1,0:T(8,128)} async-done(((f32[256,1024]{1,0:T(8,128)}), f32[256,128]{1,0:T(8,128)}) %reduce-scatter.15.cloned.1.call-update) | async-done | bytes 131088 | tf_op jit(solution)/shard_map/reduce_scatter | solution.py:247
  1130.9 10.7 all-gather.33.cloned.1.call-done
  1144.5 15.9 %all-gather.31.cloned.1.call-done = bf16[512,1024]{1,0:T(8,128)(2,1)} async-done(((bf16[128,1024]{1,0:T(8,128)(2,1)}), bf16[512,1024]{1,0:T(8,128)(2,1)}) %all-gather.31.cloned.1.call-update) | async-done | bytes 1048592 | tf_op jit(solution)/shard_map/all_gather | solution.py:277
  1163.5 25.0 %all-reduce.8 = (bf16[2,4,64]{2,1,0:T(4,128)(2,1)S(1)}, bf16[16,64]{1,0:T(8,128)(2,1)S(1)}, bf16[1024]{0:T(1024)(128)(2,1)S(1)}, bf16[1024]{0:T(1024)(128)(2,1)S...) all-reduce(f32[2,4,64]{2,1,0:T(4,128)S(1)} %pad_maximum_fusion.3, ...), channel_id=5, replica_groups=mesh['fsdp'=2,'ctx'=4,'tp'=4] {'fsdp','ctx'}, use_global_device_ids=true, to_apply=%region_24.25.clone | all-reduce | flops 7680 | bytes 46080
  1234.7 83.4 %all-reduce.20.cloned.1.call-done = bf16[2048,1024]{1,0:T(8,128)(2,1)} async-done(((bf16[2048,1024]{1,0:T(8,128)(2,1)}), bf16[2048,1024]{1,0:T(8,128)(2,1)}) %all-reduce.20.cloned.1.call-update) | async-done | bytes 4194320 | tf_op jit(solution)/shard_map/psum | solution.py:97
  1325.3 41.2 %reduce-scatter.13.cloned.1.call-done = f32[3,128,256]{1,2,0:T(8,128)} async-done(((f32[3,1024,256]{1,2,0:T(8,128)}), f32[3,128,256]{1,2,0:T(8,128)}) %reduce-scatter.13.cloned.1.call-update) | async-done | bytes 393232 | tf_op jit(solution)/shard_map/reduce_scatter | solution.py:245
  (305 shorter events, 504.6 us)
Async XLA Ops:
  7.2 32.9 %all-gather.21.cloned.1.call-start = ((), (), s32[]{:S(2)}) async-start(), calls=%async_computation.6 | async-start | bytes 2359296 | tf_op jit(solution)/shard_map/all_gather | solution.py:73
  9.5 79.2 %all-gather.25.cloned.1.call-start = ((), (), s32[]{:S(2)}) async-start(), calls=%async_computation.8 | async-start | bytes 5242880 | tf_op jit(solution)/shard_map/all_gather | solution.py:109
  54.2 71.2 %all-gather.23.cloned.1.call-start = ((), (), s32[]{:S(2)}) async-start(), calls=%async_computation.7 | async-start | bytes 5242880 | tf_op jit(solution)/shard_map/all_gather | solution.py:108
  57.9 295.6 %all-reduce.14.cloned.1.call-start = ((), (), s32[]{:S(2)}) async-start(), calls=%async_computation.9 | async-start | bytes 8388608 | tf_op jit(solution)/shard_map/psum | solution.py:97
  130.3 64.7 %copy-start.15 = (bf16[256,1024]{1,0:T(8,128)(2,1)S(1)}, bf16[256,1024]{1,0:T(8,128)(2,1)}, u32[]{:S(2)}) copy-start(bf16[256,1024]{1,0:T(8,128)(2,1)} %all_gather.84) | copy-start | bytes 1572868
  198.4 188.6 %all-gather.27.cloned.1.call-start = ((), (), s32[]{:S(2)}) async-start(), calls=%async_computation.10 | async-start | bytes 3145728 | tf_op jit(solution)/shard_map/all_gather | solution.py:79
  199.0 222.6 %all-gather.29.cloned.1.call-start = ((), (), s32[]{:S(2)}) async-start(), calls=%async_computation.11 | async-start | bytes 3145728 | tf_op jit(solution)/shard_map/all_gather | solution.py:81
  199.5 386.6 %all-reduce.16.cloned.1.call-start = ((), (), s32[]{:S(2)}) async-start(), calls=%async_computation.12 | async-start | bytes 8388608 | tf_op jit(solution)/shard_map/psum | solution.py:97
  431.0 350.2 %all-reduce.18.cloned.1.call-start = ((), (), s32[]{:S(2)}) async-start(), calls=%async_computation.13 | async-start | bytes 8388608 | tf_op jit(solution)/shard_map/psum | solution.py:97
  627.1 371.7 %reduce-scatter.19.cloned.1.call-start = ((), (), s32[]{:S(2)}) async-start(), calls=%async_computation.21 | async-start | bytes 4718592 | tf_op jit(solution)/shard_map/reduce_scatter | solution.py:253
  637.3 363.4 %reduce-scatter.17.cloned.1.call-start = ((), (), s32[]{:S(2)}) async-start(), calls=%async_computation.19 | async-start | bytes 4718592 | tf_op jit(solution)/shard_map/reduce_scatter | solution.py:251
  648.8 388.0 %reduce-scatter.9.cloned.1.call-start = ((), (), s32[]{:S(2)}) async-start(), calls=%async_computation.14 | async-start | bytes 5242880 | tf_op jit(solution)/shard_map/reduce_scatter | solution.py:208
  993.1 90.5 %reduce-scatter.11.cloned.1.call-start = ((), (), s32[]{:S(2)}) async-start(), calls=%async_computation.15 | async-start | bytes 5242880 | tf_op jit(solution)/shard_map/reduce_scatter | solution.py:211
  993.7 129.6 %reduce-scatter.15.cloned.1.call-start = ((), (), s32[]{:S(2)}) async-start(), calls=%async_computation.18 | async-start | bytes 1179648 | tf_op jit(solution)/shard_map/reduce_scatter | solution.py:247
  998.8 142.8 %all-gather.33.cloned.1.call-start = ((), (), s32[]{:S(2)}) async-start(), calls=%async_computation.22 | async-start | bytes 1310720 | tf_op jit(solution)/shard_map/all_gather | solution.py:283
  1000.6 159.7 %all-gather.31.cloned.1.call-start = ((), (), s32[]{:S(2)}) async-start(), calls=%async_computation.20 | async-start | bytes 1310720 | tf_op jit(solution)/shard_map/all_gather | solution.py:277
  1002.6 315.5 %all-reduce.20.cloned.1.call-start = ((), (), s32[]{:S(2)}) async-start(), calls=%async_computation.16 | async-start | bytes 8388608 | tf_op jit(solution)/shard_map/psum | solution.py:97
  1091.5 274.9 %reduce-scatter.13.cloned.1.call-start = ((), (), s32[]{:S(2)}) async-start(), calls=%async_computation.17 | async-start | bytes 3538944 | tf_op jit(solution)/shard_map/reduce_scatter | solution.py:245
  1099.0 64.4 %copy-start.23 = (f32[1024]{0:T(1024)S(1)}, f32[1024]{0:T(1024)}, u32[]{:S(2)}) copy-start(f32[1024]{0:T(1024)} %get-tuple-element.382) | copy-start | bytes 12292
  1099.0 64.4 %copy-start.24 = (f32[1024]{0:T(1024)S(1)}, f32[1024]{0:T(1024)}, u32[]{:S(2)}) copy-start(f32[1024]{0:T(1024)} %get-tuple-element.384) | copy-start | bytes 12292
  1099.0 64.4 %copy-start.25 = (f32[1024]{0:T(1024)S(1)}, f32[1024]{0:T(1024)}, u32[]{:S(2)}) copy-start(f32[1024]{0:T(1024)} %get-tuple-element.329) | copy-start | bytes 12292
  1099.0 64.4 %copy-start.26 = (f32[1024]{0:T(1024)S(1)}, f32[1024]{0:T(1024)}, u32[]{:S(2)}) copy-start(f32[1024]{0:T(1024)} %get-tuple-element.327) | copy-start | bytes 12292
  1099.0 64.4 %copy-start.27 = (f32[1024]{0:T(1024)S(1)}, f32[1024]{0:T(1024)}, u32[]{:S(2)}) copy-start(f32[1024]{0:T(1024)} %get-tuple-element.331) | copy-start | bytes 12292
  1099.1 219.1 %copy-start.22 = (f32[2048]{0:T(1024)S(1)}, f32[2048]{0:T(1024)}, u32[]{:S(2)}) copy-start(f32[2048]{0:T(1024)} %copy-done.21) | copy-start | bytes 24580
  (42 other events, 360.7 us)
Sparse Core Ops, SparseCore 0:
  10.1 29.8 all-gather.20
  54.3 34.4 all-gather.24
  90.9 34.4 all-gather.22
  198.5 154.9 all-reduce.13
  354.9 32.0 all-gather.26
  388.4 33.0 all-gather.28
  431.1 154.9 all-reduce.15
  627.2 153.9 all-reduce.17
  784.6 50.0 reduce-scatter.18
  837.9 51.1 reduce-scatter.16
  993.3 43.4 reduce-scatter.8
  1039.2 44.3 reduce-scatter.10
  1087.4 35.9 reduce-scatter.14
  1124.8 16.8 all-gather.32
  1143.6 16.6 all-gather.30
  1163.1 155.0 all-reduce.19
  1321.4 45.0 reduce-scatter.12
where the time goes:
time: 1390 us; the launch traced here: 1380 us
  waiting for transfers between devices  776 us (56%)
  matrix products  257 us (18%)
  blocking collectives  126 us (9%)
  other arithmetic  123 us (9%)
  local copies, waits for them, and re-layouts  85 us (6%)
  between operations  16.3 us (1%)
    psum x4, waiting for transfers between devices, finish_sum(): return lax.psum(partial_rows.astype(jnp.bfloat16), 'tp').astype(jnp.float32)  493 us
    dot_general x8, matrix products, masked_scores(): jnp.einsum('sqd,skd->sqk', query_head, key_head, preferred_element_type=j...  56.8 us
    reduce_scatter x1, waiting for transfers between devices, local(): lax.psum_scatter(grad_value_full.astype(jnp.bfloat16), 'ctx', scatter_dim...  45.3 us
    reduce_scatter x1, waiting for transfers between devices, local(): lax.psum_scatter(grad_proj_qkv, ('fsdp', 'ctx'), scatter_dimension=1, til...  41.2 us
    dot_general x4, matrix products, head_grads(): jnp.einsum('sqd,skd->sqk', grad_head, value_head, preferred_element_type=...  37.4 us
    all_gather x1, waiting for transfers between devices, local(): lax.all_gather(key_blocks, 'ctx', axis=1, tiled=True)  31.9 us
    unnamed x97, local copies, waits for them, and re-layouts  30.6 us
    reduce_scatter x1, waiting for transfers between devices, local(): lax.psum_scatter(grad_key_full.astype(jnp.bfloat16), 'ctx', scatter_dimen...  29.6 us
  transfers between devices with their start and end apart: 17, of which 15 were waited for; matrix products, arithmetic and copies ran while one was open for 21% of the time, Pallas kernels for 0%

commit v1 on v0

--- a/solution.py
+++ b/solution.py
@@ -94,7 +94,12 @@
     shift_two = shift_second.astype(jnp.float32)
 
     def finish_sum(partial_rows):
-        return lax.psum(partial_rows.astype(jnp.bfloat16), "tp").astype(jnp.float32)
+
+        def perform_sector_for(content, axis_key):
+            found_now = lax.all_gather(content, axis_name=axis_key)
+            return jnp.sum(found_now, axis=0)
+
+        return perform_sector_for(partial_rows.astype(jnp.bfloat16), "tp").astype(jnp.float32)
 
     projected = jnp.einsum("rd,kdc->krc", inputs, proj_qkv, preferred_element_type=jnp.float32)
     query_rows = (projected[0] + bias_qv[0].reshape(-1).astype(jnp.float32)).astype(jnp.bfloat16)

time: 1390 us -> 1970 us (1.42)
  waiting for transfers between devices: 776 us -> 1310 us
  other arithmetic: 123 us -> 180 us
  local copies, waits for them, and re-layouts: 85 us -> 60.3 us
    all_gather x0 -> x4, waiting for transfers between devices: none -> 1090 us  [perform_sector_for(): found_now = lax.all_gather(content, axis_name=axis_key)]
    psum x4 -> x0, waiting for transfers between devices: 493 us -> none  [finish_sum(): return lax.psum(partial_rows.astype(jnp.bfloat16), 'tp').astype(jnp.float32)]
    reduce_sum x1 -> x4, other arithmetic: 1.46 us -> 49.4 us  [perform_sector_for(): return jnp.sum(found_now, axis=0)]
    all_gather x1, waiting for transfers between devices: 31.9 us -> 8.94 us  [local(): lax.all_gather(key_blocks, 'ctx', axis=1, tiled=True)]
    while x24, local copies, waits for them, and re-layouts: 20.6 us -> 0.44 us
  transfers between devices with their start and end apart: 17 -> 17, of which waited for: 15 -> 13; matrix products, arithmetic and copies ran while one was open for 21% -> 18% of each run, Pallas kernels for 0% -> 0%
where the time goes in v1:
time: 1970 us; the launch traced here: 1960 us
  waiting for transfers between devices  1310 us (66%)
  matrix products  270 us (14%)
  other arithmetic  180 us (9%)
  blocking collectives  123 us (6%)
  local copies, waits for them, and re-layouts  60.3 us (3%)
    all_gather x4, waiting for transfers between devices, perform_sector_for(): found_now = lax.all_gather(content, axis_name=axis_key)  1090 us
    dot_general x8, matrix products, masked_scores(): jnp.einsum('sqd,skd->sqk', query_head, key_head, preferred_element_type=j...  57.4 us
    reduce_sum x4, other arithmetic, perform_sector_for(): return jnp.sum(found_now, axis=0)  49.4 us
    reduce_scatter x1, waiting for transfers between devices, local(): lax.psum_scatter(grad_value_full.astype(jnp.bfloat16), 'ctx', scatter_dim...  45.3 us
  transfers between devices with their start and end apart: 17, of which 13 were waited for; matrix products, arithmetic and copies ran while one was open for 18% of the time, Pallas kernels for 0%

profile of v1, /device:TPU:0, one launch (start us, length us, event | category | flops | bytes accessed | tf_op | source)
XLA Modules:
  0.0 1961.4 jit_solution(12715843704382153071)
XLA Ops:
  9.6 30.5 %all-gather.29.cloned.1.call-done = bf16[3,1024,256]{1,2,0:T(8,128)(2,1)} async-done(((bf16[3,512,256]{1,2,0:T(8,128)(2,1)}), bf16[3,1024,256]{1,2,0:T(8,128)(2,1)}) %all-gather.29.cloned.1.call-update) | async-done | bytes 1572880 | tf_op jit(solution)/shard_map/all_gather | solution.py:73
  90.0 31.8 %all-gather.33.cloned.1.call-done = bf16[4,2048,256]{1,2,0:T(8,128)(2,1)} async-done(((bf16[4,512,256]{1,2,0:T(8,128)(2,1)}), bf16[4,2048,256]{1,2,0:T(8,128)(2,1)}) %all-gather.33.cloned.1.call-update) | async-done | bytes 4194320 | tf_op jit(solution)/shard_map/all_gather | solution.py:114
  126.6 63.2 %while.30 = (s32[]{:T(128)}, bf16[4,4,512,64]{2,3,1,0:T(8,128)(2,1)S(1)}, f32[4,4,512,1]{2,1,3,0:T(4,128)}, f32[4,4,512,1]{2,1,3,0:T(4,128)}, bf16[4,4,512,64]{2...) while((s32[]{:T(128)}, ...), condition=%wide.region_3.4_spmd.clone, body=%wide.region_0.3_spmd.clone.sunk | while | flops 1136783360 | bytes 53151856 | solution.py:135
  215.5 267.8 %all-gather.43.cloned.1.call-done = bf16[8192,1024]{1,0:T(8,128)(2,1)} async-done(((bf16[2048,1024]{1,0:T(8,128)(2,1)}), bf16[8192,1024]{1,0:T(8,128)(2,1)}) %all-gather.43.cloned.1.call-update) | async-done | bytes 16777232 | tf_op jit(solution)/shard_map/all_gather | solution.py:99
  483.3 12.6 reduce_sum.232
  516.0 10.9 multiply_convert_fusion.1
  526.9 23.6 %all-gather.37.cloned.1.call-done = bf16[1024,1024]{1,0:T(8,128)(2,1)} async-done(((bf16[1024,512]{1,0:T(8,128)(2,1)}), bf16[1024,1024]{1,0:T(8,128)(2,1)}) %all-gather.37.cloned.1.call-update) | async-done | bytes 2097168 | tf_op jit(solution)/shard_map/all_gather | solution.py:81
  569.0 277.9 %all-gather.45.cloned.1.call-done = bf16[8192,1024]{1,0:T(8,128)(2,1)} async-done(((bf16[2048,1024]{1,0:T(8,128)(2,1)}), bf16[8192,1024]{1,0:T(8,128)(2,1)}) %all-gather.45.cloned.1.call-update) | async-done | bytes 16777232 | tf_op jit(solution)/shard_map/all_gather | solution.py:99
  846.8 12.1 reduce_sum.235
  877.2 12.5 convert_reduce_fusion.1
  898.5 11.5 fusion.63
  914.5 11.7 fusion.86
  926.4 256.7 %all-gather.47.cloned.1.call-done = bf16[8192,1024]{1,0:T(8,128)(2,1)} async-done(((bf16[2048,1024]{1,0:T(8,128)(2,1)}), bf16[8192,1024]{1,0:T(8,128)(2,1)}) %all-gather.47.cloned.1.call-update) | async-done | bytes 16777232 | tf_op jit(solution)/shard_map/all_gather | solution.py:99
  1183.2 12.3 reduce_sum.280
  1195.5 15.2 multiply_reduce_fusion.1
  1228.5 171.5 %while.31 = (s32[]{:T(128)}, bf16[4,4,512,64]{2,3,1,0:T(8,128)(2,1)}, bf16[4,4,2048,64]{2,3,0,1:T(8,128)(2,1)}, bf16[4,4,2048,64]{2,3,0,1:T(8,128)(2,1)}, bf16[4...) while((s32[]{:T(128)}, ...), condition=%wide.region_17.18_spmd.clone, body=%wide.region_15.17_spmd.clone.sunk | while | flops 2731276288 | bytes 177057008 | solution.py:207
  1248.7 10.0 multiply_convert_fusion.3
  1408.2 35.9 %reduce-scatter.9.cloned.1.call-done = bf16[4,512,256]{1,2,0:T(8,128)(2,1)} async-done(((bf16[4,2048,256]{1,2,0:T(8,128)(2,1)}), bf16[4,512,256]{1,2,0:T(8,128)(2,1)}) %reduce-scatter.9.cloned.1.call-update) | async-done | bytes 1048592 | tf_op jit(solution)/shard_map/reduce_scatter | solution.py:213
  1445.6 45.3 %reduce-scatter.11.cloned.1.call-done = bf16[4,512,256]{1,2,0:T(8,128)(2,1)} async-done(((bf16[4,2048,256]{1,2,0:T(8,128)(2,1)}), bf16[4,512,256]{1,2,0:T(8,128)(2,1)}) %reduce-scatter.11.cloned.1.call-update) | async-done | bytes 1048592 | tf_op jit(solution)/shard_map/reduce_scatter | solution.py:216
  1513.4 15.2 all-gather.39.cloned.1.call-done
  1531.5 286.0 %all-gather.49.cloned.1.call-done = bf16[8192,1024]{1,0:T(8,128)(2,1)} async-done(((bf16[2048,1024]{1,0:T(8,128)(2,1)}), bf16[8192,1024]{1,0:T(8,128)(2,1)}) %all-gather.49.cloned.1.call-update) | async-done | bytes 16777232 | tf_op jit(solution)/shard_map/all_gather | solution.py:99
  1817.5 12.4 reduce_sum.284
  1840.1 24.8 %reduce-scatter.13.cloned.1.call-done = f32[3,128,256]{1,2,0:T(8,128)} async-done(((f32[3,1024,256]{1,2,0:T(8,128)}), f32[3,128,256]{1,2,0:T(8,128)}) %reduce-scatter.13.cloned.1.call-update) | async-done | bytes 393232 | tf_op jit(solution)/shard_map/reduce_scatter | solution.py:250
  1876.3 24.2 %all-reduce.8 = (bf16[2,4,64]{2,1,0:T(4,128)(2,1)S(1)}, bf16[16,64]{1,0:T(8,128)(2,1)S(1)}, bf16[1024]{0:T(1024)(128)(2,1)S(1)}, bf16[1024]{0:T(1024)(128)(2,1)S...) all-reduce(f32[2,4,64]{2,1,0:T(4,128)S(1)} %pad_maximum_fusion.3, ...), channel_id=9, replica_groups=mesh['fsdp'=2,'ctx'=4,'tp'=4] {'fsdp','ctx'}, use_global_device_ids=true, to_apply=%region_24.25.clone | all-reduce | flops 7680 | bytes 46080
  (328 shorter events, 503.7 us)
Async XLA Ops:
  7.2 32.9 %all-gather.29.cloned.1.call-start = ((), (), s32[]{:S(2)}) async-start(), calls=%async_computation.6 | async-start | bytes 2359296 | tf_op jit(solution)/shard_map/all_gather | solution.py:73
  9.5 75.6 %all-gather.31.cloned.1.call-start = ((), (), s32[]{:S(2)}) async-start(), calls=%async_computation.7 | async-start | bytes 5242880 | tf_op jit(solution)/shard_map/all_gather | solution.py:113
  50.6 71.2 %all-gather.33.cloned.1.call-start = ((), (), s32[]{:S(2)}) async-start(), calls=%async_computation.8 | async-start | bytes 5242880 | tf_op jit(solution)/shard_map/all_gather | solution.py:114
  64.9 418.4 %all-gather.43.cloned.1.call-start = ((), (), s32[]{:S(2)}) async-start(), calls=%async_computation.19 | async-start | bytes 20971520 | tf_op jit(solution)/shard_map/all_gather | solution.py:99
  190.7 15.7 copy-start.35
  190.7 20.1 %copy-start.30 = (bf16[16,32]{1,0:T(8,128)(2,1)S(1)}, bf16[16,32]{1,0:T(8,128)(2,1)}, u32[]{:S(2)}) copy-start(bf16[16,32]{1,0:T(8,128)(2,1)} %param.28) | copy-start | bytes 3076
  196.4 319.6 %all-gather.35.cloned.1.call-start = ((), (), s32[]{:S(2)}) async-start(), calls=%async_computation.9 | async-start | bytes 3145728 | tf_op jit(solution)/shard_map/all_gather | solution.py:79
  197.0 353.5 %all-gather.37.cloned.1.call-start = ((), (), s32[]{:S(2)}) async-start(), calls=%async_computation.10 | async-start | bytes 3145728 | tf_op jit(solution)/shard_map/all_gather | solution.py:81
  197.6 649.3 %all-gather.45.cloned.1.call-start = ((), (), s32[]{:S(2)}) async-start(), calls=%async_computation.20 | async-start | bytes 20971520 | tf_op jit(solution)/shard_map/all_gather | solution.py:99
  559.9 623.2 %all-gather.47.cloned.1.call-start = ((), (), s32[]{:S(2)}) async-start(), calls=%async_computation.21 | async-start | bytes 20971520 | tf_op jit(solution)/shard_map/all_gather | solution.py:99
  898.1 502.6 %reduce-scatter.19.cloned.1.call-start = ((), (), s32[]{:S(2)}) async-start(), calls=%async_computation.17 | async-start | bytes 4718592 | tf_op jit(solution)/shard_map/reduce_scatter | solution.py:258
  910.0 492.5 %reduce-scatter.17.cloned.1.call-start = ((), (), s32[]{:S(2)}) async-start(), calls=%async_computation.15 | async-start | bytes 4718592 | tf_op jit(solution)/shard_map/reduce_scatter | solution.py:256
  926.2 517.9 %reduce-scatter.9.cloned.1.call-start = ((), (), s32[]{:S(2)}) async-start(), calls=%async_computation.11 | async-start | bytes 5242880 | tf_op jit(solution)/shard_map/reduce_scatter | solution.py:213
  1400.0 90.9 %reduce-scatter.11.cloned.1.call-start = ((), (), s32[]{:S(2)}) async-start(), calls=%async_computation.12 | async-start | bytes 5242880 | tf_op jit(solution)/shard_map/reduce_scatter | solution.py:216
  1400.6 110.0 %all-gather.41.cloned.1.call-start = ((), (), s32[]{:S(2)}) async-start(), calls=%async_computation.18 | async-start | bytes 1310720 | tf_op jit(solution)/shard_map/all_gather | solution.py:288
  1402.5 126.2 %all-gather.39.cloned.1.call-start = ((), (), s32[]{:S(2)}) async-start(), calls=%async_computation.16 | async-start | bytes 1310720 | tf_op jit(solution)/shard_map/all_gather | solution.py:282
  1404.4 413.1 %all-gather.49.cloned.1.call-start = ((), (), s32[]{:S(2)}) async-start(), calls=%async_computation.22 | async-start | bytes 20971520 | tf_op jit(solution)/shard_map/all_gather | solution.py:99
  1500.8 364.1 %reduce-scatter.13.cloned.1.call-start = ((), (), s32[]{:S(2)}) async-start(), calls=%async_computation.13 | async-start | bytes 3538944 | tf_op jit(solution)/shard_map/reduce_scatter | solution.py:250
  1508.6 438.2 %reduce-scatter.15.cloned.1.call-start = ((), (), s32[]{:S(2)}) async-start(), calls=%async_computation.14 | async-start | bytes 1179648 | tf_op jit(solution)/shard_map/reduce_scatter | solution.py:252
  1837.2 39.1 %copy-start.25 = (f32[1024]{0:T(1024)S(1)}, f32[1024]{0:T(1024)}, u32[]{:S(2)}) copy-start(f32[1024]{0:T(1024)} %get-tuple-element.329) | copy-start | bytes 12292
  1837.2 39.1 %copy-start.26 = (f32[1024]{0:T(1024)S(1)}, f32[1024]{0:T(1024)}, u32[]{:S(2)}) copy-start(f32[1024]{0:T(1024)} %get-tuple-element.330) | copy-start | bytes 12292
  1837.2 39.1 %copy-start.27 = (f32[1024]{0:T(1024)S(1)}, f32[1024]{0:T(1024)}, u32[]{:S(2)}) copy-start(f32[1024]{0:T(1024)} %get-tuple-element.334) | copy-start | bytes 12292
  1837.2 39.1 %copy-start.28 = (f32[1024]{0:T(1024)S(1)}, f32[1024]{0:T(1024)}, u32[]{:S(2)}) copy-start(f32[1024]{0:T(1024)} %get-tuple-element.402) | copy-start | bytes 12292
  1837.2 39.0 %copy-start.29 = (f32[1024]{0:T(1024)S(1)}, f32[1024]{0:T(1024)}, u32[]{:S(2)}) copy-start(f32[1024]{0:T(1024)} %get-tuple-element.404) | copy-start | bytes 12292
  (47 other events, 338.2 us)
Sparse Core Ops, SparseCore 0:
  10.1 29.8 all-gather.28
  50.7 34.4 all-gather.30
  87.3 34.4 all-gather.32
  196.5 286.7 all-gather.42
  484.7 31.2 all-gather.34
  517.4 33.0 all-gather.36
  560.1 286.7 all-gather.44
  898.2 284.9 all-gather.46
  1186.5 49.2 reduce-scatter.18
  1239.0 51.1 reduce-scatter.16
  1400.1 43.9 reduce-scatter.8
  1446.5 44.3 reduce-scatter.10
  1493.1 16.8 all-gather.40
  1511.9 16.7 all-gather.38
  1530.7 286.7 all-gather.48
  1820.7 44.2 reduce-scatter.12
  1868.0 36.0 reduce-scatter.14
